TPU v7x, 128 devices: a whole 4x4x4 slice. The times are simulated.
128 devices in a mesh: grp: 8 (over y, x_lo), bal: 16 (over x_hi, z, core).
Axes of the slice: x: 4 (x_hi: 2, x_lo: 2; x = x_hi * 2 + x_lo), y: 4, z: 4, core: 2. Of those that a mesh axis runs over, the one named last changes fastest.
Arguments:
- events: bfloat16 [8, 8192, 512], P('grp', 'bal'), may hold values from -6 to 6
- cotangent: bfloat16 [8, 8192, 512], P('grp', 'bal'), may hold values from -6 to 6
- lengths: int32 [8, 16], P('grp'), may hold values from 1 to 16, as said below
- gain_in: float32 [512], replicated, may hold values from 0.1 to 1.9
- w_proj: bfloat16 [512, 2048], replicated, may hold values from -0.25 to 0.25
- gain_attn: float32 [512], replicated, may hold values from 0.1 to 1.9
- w_out: bfloat16 [512, 512], replicated, may hold values from -0.25 to 0.25
Outputs:
- d_x: bfloat16 [8, 8192, 512], P('grp', 'bal')
- grad_proj: float32 [512, 2048], replicated
- grad_out: float32 [512, 512], replicated
- grad_gain_in: float32 [512], replicated
- grad_gain_attn: float32 [512], replicated
Inputs may be any that keep to these rules, and one draw needn't show every extreme that they name: A group's 16 lengths count blocks of 64 events and sum to 128; in every group one length equals 16.
All inputs are finite; a program needn't handle non-finite values.
Results may differ from a plain program's by a relative error of at most 0.013.
Values may be sent and summed in bfloat16 or wider, within the bound.
No kernel may reach another device: no remote copies, remote signals or barrier semaphores. Data moves between devices by JAX's collectives and lax.ppermute only.
A program may use at most 256 MiB of HBM per device.

v0:
```python
import math
import jax
import jax.numpy as jnp
from jax import lax
from jax.sharding import PartitionSpec as P

HEADS = 8
BLOCK = 64
LEN_BLK = 16
epsilon = 1e-06


def norm_rows(values):
    mean_value = jnp.mean(values, axis=-1, keepdims=True)
    centred = values - mean_value
    rstd = lax.rsqrt(jnp.mean(centred * centred, axis=-1, keepdims=True) + epsilon)
    return (centred * rstd, rstd)


def silu_slope(values):
    sigma = jax.nn.sigmoid(values)
    return sigma * (1.0 + values * (1.0 - sigma))


def norm_back(grad, normed, rstd):
    return rstd * (
        grad
        - jnp.mean(grad, axis=-1, keepdims=True)
        - normed * jnp.mean(grad * normed, axis=-1, keepdims=True)
    )


def contract_rows(left, right):
    return lax.dot_general(
        left, right, (((0,), (0,)), ((), ())), preferred_element_type=jnp.float32
    )


def contract_cols(left, right):
    return lax.dot_general(
        left, right, (((1,), (1,)), ((), ())), preferred_element_type=jnp.float32
    )


def project_rows(rows, gain_in, w_proj):
    normed, rstd_in = norm_rows(rows.astype(jnp.float32))
    scaled = (normed * gain_in).astype(jnp.bfloat16)
    hidden = jnp.dot(scaled, w_proj, preferred_element_type=jnp.float32)
    active = jax.nn.silu(hidden).astype(jnp.bfloat16)
    return (normed, rstd_in, scaled, hidden, active)


def output_rows(attn, upper, grads_out, gain_attn, w_out):
    normed, rstd = norm_rows(attn.astype(jnp.float32))
    upper_wide = upper.astype(jnp.float32)
    mixed = (normed * gain_attn * upper_wide).astype(jnp.bfloat16)
    d_mixed = contract_cols(grads_out, w_out)
    d_upper = d_mixed * normed * gain_attn
    d_attn = norm_back(d_mixed * gain_attn * upper_wide, normed, rstd).astype(jnp.bfloat16)
    out_term = contract_rows(mixed, grads_out)
    gain_term = jnp.sum(d_mixed * normed * upper_wide, axis=0)
    return (d_upper, d_attn, out_term, gain_term)


def input_rows(grads_out, d_act, hidden, normed, rstd_in, scaled, gain_in, w_proj):
    d_hidden = (d_act * silu_slope(hidden)).astype(jnp.bfloat16)
    proj_term = contract_rows(scaled, d_hidden)
    d_scaled = contract_cols(d_hidden, w_proj)
    d_rows = (
        grads_out.astype(jnp.float32) + norm_back(d_scaled * gain_in, normed, rstd_in)
    ).astype(jnp.bfloat16)
    gain_term = jnp.sum(d_scaled * normed, axis=0)
    return (d_rows, proj_term, gain_term)


def attend_forward(query, keys, values, allowed):
    head_width = query.shape[1] // HEADS
    scale = head_width ** (-0.5)
    outputs = []
    for head in range(HEADS):
        columns = slice(head * head_width, (head + 1) * head_width)
        scores = contract_cols(query[:, columns], keys[:, columns]) * scale
        weights = (jax.nn.silu(scores) * allowed).astype(jnp.bfloat16)
        outputs.append(jnp.dot(weights, values[:, columns], preferred_element_type=jnp.float32))
    return jnp.concatenate(outputs, axis=1).astype(jnp.bfloat16)


def attend_backward(query, keys, values, grad_attn, allowed):
    head_width = query.shape[1] // HEADS
    scale = head_width ** (-0.5)
    grads_query, grads_keys, grads_values = ([], [], [])
    for head in range(HEADS):
        columns = slice(head * head_width, (head + 1) * head_width)
        query_head = query[:, columns]
        key_head = keys[:, columns]
        grad_head = grad_attn[:, columns]
        scores = contract_cols(query_head, key_head) * scale
        weights = (jax.nn.silu(scores) * allowed).astype(jnp.bfloat16)
        grad_weights = contract_cols(grad_head, values[:, columns])
        grad_scores = (grad_weights * silu_slope(scores) * allowed).astype(jnp.bfloat16)
        grads_values.append(contract_rows(weights, grad_head).astype(jnp.bfloat16))
        grads_query.append(
            (jnp.dot(grad_scores, key_head, preferred_element_type=jnp.float32) * scale).astype(
                jnp.bfloat16
            )
        )
        grads_keys.append((contract_rows(grad_scores, query_head) * scale).astype(jnp.bfloat16))
    return (
        jnp.concatenate(grads_query, axis=1),
        jnp.concatenate(grads_keys, axis=1),
        jnp.concatenate(grads_values, axis=1),
    )


def lookup(table, positions):
    entries = jnp.arange(table.shape[0], dtype=jnp.int32)
    picked = jnp.where(entries[None, :] == positions[:, None], table[None, :], 0)
    return jnp.sum(picked, axis=1)


def regroup(table, rows):
    blocks = rows.reshape(table.shape[1], -1)
    moved = jnp.dot(table, blocks, preferred_element_type=jnp.float32)
    return moved.astype(jnp.bfloat16).reshape(-1, rows.shape[1])


def pack_histories(seq_lengths):

    def advance(state, length_now):
        device_rank, held_blocks = state
        fresh = held_blocks + length_now > LEN_BLK
        device_rank = device_rank + fresh.astype(jnp.int32)
        held_blocks = jnp.where(fresh, 0, held_blocks) + length_now
        return ((device_rank, held_blocks), device_rank)

    start_state = (jnp.int32(0), jnp.int32(0))
    final_state, ranks = lax.scan(advance, start_state, seq_lengths)
    return ranks


def held_tiles_map(tile_fn, live_tiles, inputs, tile_rows):
    count = inputs[0].shape[0] // tile_rows
    pieces = tuple((array.reshape((count, tile_rows) + array.shape[1:]) for array in inputs))

    def blank_fn(parts):
        return jax.tree.map(jnp.zeros_like, tile_fn(parts))

    def each_tile(item):
        position, parts = item
        return lax.cond(position < live_tiles, tile_fn, blank_fn, parts)

    return lax.map(each_tile, (jnp.arange(count, dtype=jnp.int32), pieces))


def flatten_tiles(array):
    return array.reshape((-1,) + array.shape[2:])


def whole_layer(rows, grads_out, allowed, live_tiles, tile_rows, gain_in, w_proj, gain_attn, w_out):
    width = rows.shape[1]
    first = held_tiles_map(
        lambda parts: project_rows(parts[0], gain_in, w_proj), live_tiles, (rows,), tile_rows
    )
    normed, rstd_in, scaled, hidden, active = jax.tree.map(flatten_tiles, first)
    upper = active[:, :width]
    values = active[:, width : 2 * width]
    query = active[:, 2 * width : 3 * width]
    keys = active[:, 3 * width :]
    attn = attend_forward(query, keys, values, allowed)
    second = held_tiles_map(
        lambda parts: output_rows(parts[0], parts[1], parts[2], gain_attn, w_out),
        live_tiles,
        (attn, upper, grads_out),
        tile_rows,
    )
    d_upper = flatten_tiles(second[0])
    d_attn = flatten_tiles(second[1])
    out_term = jnp.sum(second[2], axis=0)
    gain_attn_term = jnp.sum(second[3], axis=0)
    d_query, d_keys, d_values = attend_backward(query, keys, values, d_attn, allowed)
    d_act = jnp.concatenate(
        [
            d_upper,
            d_values.astype(jnp.float32),
            d_query.astype(jnp.float32),
            d_keys.astype(jnp.float32),
        ],
        axis=1,
    )
    third = held_tiles_map(
        lambda parts: input_rows(
            parts[0], parts[1], parts[2], parts[3], parts[4], parts[5], gain_in, w_proj
        ),
        live_tiles,
        (grads_out, d_act, hidden, normed, rstd_in, scaled),
        tile_rows,
    )
    d_rows = flatten_tiles(third[0])
    proj_term = jnp.sum(third[1], axis=0)
    gain_in_term = jnp.sum(third[2], axis=0)
    return (d_rows, (proj_term, out_term, gain_in_term, gain_attn_term))


def per_device(events, cotangent, lengths, gain_in, w_proj, gain_attn, w_out):
    peers = lax.axis_size("bal")
    own_index = lax.axis_index("bal")
    local_rows = events[0]
    local_grads = cotangent[0]
    local_blocks = local_rows.shape[0] // BLOCK
    slots = LEN_BLK // peers
    seq_lengths = lengths[0]
    targets = pack_histories(seq_lengths)
    ends = jnp.cumsum(seq_lengths)
    device_ids = jnp.arange(peers, dtype=jnp.int32)
    range_starts = jnp.sum(
        jnp.where(targets[None, :] < device_ids[:, None], seq_lengths[None, :], 0), axis=1
    )
    range_sizes = jnp.sum(
        jnp.where(targets[None, :] == device_ids[:, None], seq_lengths[None, :], 0), axis=1
    )
    flat_blocks = own_index + peers * jnp.arange(local_blocks, dtype=jnp.int32)
    owner_seq = jnp.sum((ends[None, :] <= flat_blocks[:, None]).astype(jnp.int32), axis=1)
    owner = lookup(targets, owner_seq)
    slot_index = (flat_blocks - lookup(range_starts, owner)) // peers
    slot_ids = jnp.arange(peers * slots, dtype=jnp.int32)
    send_table = (slot_ids[:, None] == (owner * slots + slot_index)[None, :]).astype(jnp.bfloat16)
    mine_start = lookup(range_starts, own_index[None])[0]
    mine_size = lookup(range_sizes, own_index[None])[0]
    block_order = jnp.arange(LEN_BLK, dtype=jnp.int32)
    from_slot = (mine_start + block_order) % peers * slots + block_order // peers
    take_table = (from_slot[:, None] == slot_ids[None, :]).astype(jnp.bfloat16)
    return_table = jnp.transpose(take_table)
    home_table = jnp.transpose(send_table)
    block_seq = jnp.sum(
        (ends[None, :] <= (mine_start + block_order)[:, None]).astype(jnp.int32), axis=1
    )
    block_seq = jnp.where(block_order < mine_size, block_seq, -1)
    row_seq = jnp.repeat(block_seq, BLOCK)
    positions = jnp.arange(LEN_BLK * BLOCK, dtype=jnp.int32)
    allowed = (
        (row_seq[:, None] == row_seq[None, :])
        & (row_seq[:, None] >= 0)
        & (positions[None, :] <= positions[:, None])
    ).astype(jnp.float32)
    tile_blocks = math.gcd(LEN_BLK, max(1, 256 // BLOCK))
    live_tiles = (mine_size + tile_blocks - 1) // tile_blocks
    got_rows, got_grads = (
        lax.all_to_all(
            regroup(send_table, local_rows), "bal", split_axis=0, concat_axis=0, tiled=True
        ),
        lax.all_to_all(
            regroup(send_table, local_grads), "bal", split_axis=0, concat_axis=0, tiled=True
        ),
    )
    held_rows = regroup(take_table, got_rows)
    held_grads = regroup(take_table, got_grads)
    d_held, terms = whole_layer(
        held_rows,
        held_grads,
        allowed,
        live_tiles,
        tile_blocks * BLOCK,
        gain_in,
        w_proj,
        gain_attn,
        w_out,
    )
    came_back = lax.all_to_all(
        regroup(return_table, d_held), "bal", split_axis=0, concat_axis=0, tiled=True
    )
    d_rows = regroup(home_table, came_back)
    sums = lax.psum((terms[0], terms[1], terms[2], terms[3]), ("grp", "bal"))
    divisor = float(lax.axis_size("grp") * peers)
    return (
        d_rows[None],
        sums[0] / divisor,
        sums[1] / divisor,
        sums[2] / divisor,
        sums[3] / divisor,
    )


def solution(mesh):
    placed = (P("grp", "bal", None), P("grp", "bal", None), P("grp", None), P(), P(), P(), P())
    return jax.shard_map(
        per_device,
        mesh=mesh,
        in_specs=placed,
        out_specs=(P("grp", "bal", None), P(), P(), P(), P()),
        check_vma=False,
    )
```

profile of v0, /device:TPU:1, one launch (start us, length us, event | category | flops | bytes accessed | tf_op | source)
XLA Modules:
  0.0 636.9 jit_solution(15162623421532527161)
XLA Ops:
  7.2 42.6 %while.66 = (s32[]{:T(128)}, s32[]{:T(128)}, s32[]{:T(128)}, s32[16]{0:T(128)S(1)}, s32[16]{0:T(128)}) while((s32[]{:T(128)}, s32[]{:T(128)}, s32[]{:T(128)}, s32[16]{0:T(128)S(1)}, s32[16]{0:T(128)}) %tuple.198), condition=%wide.region_3.4_spmd.clone, body=%wide.region_2.3_spmd.sunk.clone | while | flops 8 | bytes 148 | solution.py:137
  55.1 9.3 %all-to-all-start.1 = ((bf16[16,64,512]{2,1,0:T(8,128)(2,1)}), bf16[16,64,512]{2,1,0:T(8,128)(2,1)S(1)}, u32[]{:S(2)}, u32[]{:S(2)}) async-start(bf16[16,64,512]{2,1,0:T(8,128)(2,1)} %bitcast.70), calls=%async_computation.1 | async-start | bytes 2097152 | tf_op jit(solution)/shard_map/all_to_all | solution.py:248
  70.0 11.6 %all-to-all-done.1 = bf16[16,64,512]{2,1,0:T(8,128)(2,1)S(1)} async-done(((bf16[16,64,512]{2,1,0:T(8,128)(2,1)}), bf16[16,64,512]{2,1,0:T(8,128)(2,1)S(1)}, u32[]{:S(2)}, u32[]{:S(2)}) %all-to-all-start.1) | async-done | bytes 1048608 | tf_op jit(solution)/shard_map/all_to_all | solution.py:248
  81.6 5.0 all-to-all-start
  91.9 70.2 %while.67 = (s32[]{:T(128)}, f32[4,256,512]{2,1,0:T(8,128)}, f32[4,256,1]{1,2,0:T(1,128)}, bf16[4,256,512]{2,1,0:T(8,128)(2,1)}, f32[4,256,2048]{2,1,0:T(8,128)}...) while((s32[]{:T(128)}, f32[4,256,512]{2,1,0:T(8,128)}, ...), condition=%wide.region_16.17_spmd.clone, body=%wide.region_11.16_spmd.sunk.clone | while | flops 541589760 | bytes 17060060 | solution.py:152
  93.2 9.2 %conditional.9 = (f32[1,256,512]{2,1,0:T(8,128)S(1)}, f32[1,256,1]{1,2,0:T(1,128)}, bf16[1,256,512]{2,1,0:T(8,128)(2,1)S(1)}, f32[1,256,2048]{2,1,0:T(8,128)}, bf16[1,256,2048]{2,1,0:T(8,128)(2,1)S(1)}) conditional(s32[]{:T(128)} %convert_element_type.475, () %tuple.157, (bf16[4,256,512]{2,1,0:T(8,128)(2,1)}, s32[]{:T(128)}, f32[512]{0:T(512)S(1)}, ...), branch_computations={%region_12.12_spmd, %region_13.15_spmd} | conditional | flops 541589760 | bytes 9190964 | solution.py:150
  96.0 3.1 fusion.8
  102.4 3.2 constant_dynamic-update-slice_fusion.33
  110.8 9.2 %conditional.9 = (f32[1,256,512]{2,1,0:T(8,128)S(1)}, f32[1,256,1]{1,2,0:T(1,128)}, bf16[1,256,512]{2,1,0:T(8,128)(2,1)S(1)}, f32[1,256,2048]{2,1,0:T(8,128)}, bf16[1,256,2048]{2,1,0:T(8,128)(2,1)S(1)}) conditional(s32[]{:T(128)} %convert_element_type.475, () %tuple.157, (bf16[4,256,512]{2,1,0:T(8,128)(2,1)}, s32[]{:T(128)}, f32[512]{0:T(512)S(1)}, ...), branch_computations={%region_12.12_spmd, %region_13.15_spmd} | conditional | flops 541589760 | bytes 9190964 | solution.py:150
  113.6 3.1 fusion.8
  120.0 3.1 constant_dynamic-update-slice_fusion.33
  128.4 9.2 %conditional.9 = (f32[1,256,512]{2,1,0:T(8,128)S(1)}, f32[1,256,1]{1,2,0:T(1,128)}, bf16[1,256,512]{2,1,0:T(8,128)(2,1)S(1)}, f32[1,256,2048]{2,1,0:T(8,128)}, bf16[1,256,2048]{2,1,0:T(8,128)(2,1)S(1)}) conditional(s32[]{:T(128)} %convert_element_type.475, () %tuple.157, (bf16[4,256,512]{2,1,0:T(8,128)(2,1)}, s32[]{:T(128)}, f32[512]{0:T(512)S(1)}, ...), branch_computations={%region_12.12_spmd, %region_13.15_spmd} | conditional | flops 541589760 | bytes 9190964 | solution.py:150
  131.2 3.1 fusion.8
  137.6 3.2 constant_dynamic-update-slice_fusion.33
  145.9 9.2 %conditional.9 = (f32[1,256,512]{2,1,0:T(8,128)S(1)}, f32[1,256,1]{1,2,0:T(1,128)}, bf16[1,256,512]{2,1,0:T(8,128)(2,1)S(1)}, f32[1,256,2048]{2,1,0:T(8,128)}, bf16[1,256,2048]{2,1,0:T(8,128)(2,1)S(1)}) conditional(s32[]{:T(128)} %convert_element_type.475, () %tuple.157, (bf16[4,256,512]{2,1,0:T(8,128)(2,1)}, s32[]{:T(128)}, f32[512]{0:T(512)S(1)}, ...), branch_computations={%region_12.12_spmd, %region_13.15_spmd} | conditional | flops 541589760 | bytes 9190964 | solution.py:150
  148.8 3.1 fusion.8
  155.2 3.1 constant_dynamic-update-slice_fusion.33
  162.2 3.7 fusion.113
  165.9 3.7 fusion.120
  169.6 3.7 fusion.127
  173.3 3.9 fusion.134
  177.2 3.7 fusion.141
  180.9 3.8 fusion.148
  186.4 19.1 %select_convert_fusion.8 = (bf16[1024,1024]{1,0:T(8,128)(2,1)S(1)}, bf16[1024,1024]{1,0:T(8,128)(2,1)}, bf16[1024,1024]{1,0:T(8,128)(2,1)}, bf16[1024,1024]{1,0:...) fusion(pred[1024]{0:T(1024)(128)(4,1)S(1)} %broadcast_compare_f, ...), kind=kOutput, calls=%fused_computation.122 | convolution fusion | flops 197132288 | bytes 50865152 | tf_op jit(solution)/shard_map/dot_general | solution.py:40
  237.3 35.1 %while.68 = (s32[]{:T(128)}, f32[4,256,512]{2,1,0:T(8,128)}, bf16[4,256,512]{2,1,0:T(8,128)(2,1)}, f32[4,512,512]{2,1,0:T(8,128)}, f32[4,512]{1,0:T(4,128)S(1)},...) while((s32[]{:T(128)}, f32[4,256,512]{2,1,0:T(8,128)}, ...), condition=%wide.region_25.26_spmd.clone, body=%wide.region_17.25_spmd.sunk.clone | while | flops 273415936 | bytes 9736943 | solution.py:152
  238.5 4.9 conditional.10
  247.3 4.9 conditional.10
  256.1 4.9 conditional.10
  264.8 4.9 conditional.10
  282.7 5.2 select_convert_fusion.1
  288.0 4.9 select_convert_fusion.2
  292.9 4.8 select_convert_fusion.3
  297.7 4.9 select_convert_fusion.4
  302.6 4.8 select_convert_fusion.5
  307.4 4.9 select_convert_fusion.6
  312.3 4.8 select_convert_fusion.7
  317.2 4.9 select_convert_fusion
  329.9 2.4 fusion.76
  338.4 2.4 fusion.74
  347.5 2.5 fusion.72
  372.0 5.6 pad_maximum_fusion
  377.8 67.9 %while.69 = (s32[]{:T(128)}, bf16[4,256,512]{2,1,0:T(8,128)(2,1)S(1)}, f32[4,512,2048]{2,1,0:T(8,128)}, f32[4,512]{1,0:T(4,128)S(1)}, s32[4]{0:T(128)S(1)}, /*in...) while((s32[]{:T(128)}, ...), condition=%wide.region_32.33_spmd.clone, body=%wide.region_26.32_spmd.sunk.clone | while | flops 1085013504 | bytes 26500880 | solution.py:152
  379.3 10.9 %conditional.11 = (bf16[1,256,512]{2,1,0:T(8,128)(2,1)S(1)}, f32[1,512,2048]{2,1,0:T(8,128)}, f32[1,512]{1,0:T(1,128)S(1)}) conditional(s32[]{:T(128)} %convert_element_type.477, () %tuple.167, (bf16[4,256,512]{2,1,0:T(8,128)(2,1)}, s32[]{:T(128)}, f32[4,256,1]{1,2,0:T(1,128)}, f32[4,256,2048]{2,1,0:T(8,128)}, f32[4,256,2048]{2,1,0:T(8,128)}, ...), branch_computations={%region_27.27_spmd, %region_28.31_spmd} | conditional | flops 1085013504 | bytes 17583136 | solution.py:150
  379.3 3.4 fusion.62
  384.7 5.5 convolution_bitcast_fusion.1
  390.2 4.6 constant_dynamic-update-slice_fusion.39
  396.1 10.9 %conditional.11 = (bf16[1,256,512]{2,1,0:T(8,128)(2,1)S(1)}, f32[1,512,2048]{2,1,0:T(8,128)}, f32[1,512]{1,0:T(1,128)S(1)}) conditional(s32[]{:T(128)} %convert_element_type.477, () %tuple.167, (bf16[4,256,512]{2,1,0:T(8,128)(2,1)}, s32[]{:T(128)}, f32[4,256,1]{1,2,0:T(1,128)}, f32[4,256,2048]{2,1,0:T(8,128)}, f32[4,256,2048]{2,1,0:T(8,128)}, ...), branch_computations={%region_27.27_spmd, %region_28.31_spmd} | conditional | flops 1085013504 | bytes 17583136 | solution.py:150
  396.2 3.4 fusion.62
  401.6 5.5 convolution_bitcast_fusion.1
  407.1 4.7 constant_dynamic-update-slice_fusion.39
  413.1 11.0 %conditional.11 = (bf16[1,256,512]{2,1,0:T(8,128)(2,1)S(1)}, f32[1,512,2048]{2,1,0:T(8,128)}, f32[1,512]{1,0:T(1,128)S(1)}) conditional(s32[]{:T(128)} %convert_element_type.477, () %tuple.167, (bf16[4,256,512]{2,1,0:T(8,128)(2,1)}, s32[]{:T(128)}, f32[4,256,1]{1,2,0:T(1,128)}, f32[4,256,2048]{2,1,0:T(8,128)}, f32[4,256,2048]{2,1,0:T(8,128)}, ...), branch_computations={%region_27.27_spmd, %region_28.31_spmd} | conditional | flops 1085013504 | bytes 17583136 | solution.py:150
  413.1 3.4 fusion.62
  418.5 5.5 convolution_bitcast_fusion.1
  424.0 4.7 constant_dynamic-update-slice_fusion.39
  430.0 11.0 %conditional.11 = (bf16[1,256,512]{2,1,0:T(8,128)(2,1)S(1)}, f32[1,512,2048]{2,1,0:T(8,128)}, f32[1,512]{1,0:T(1,128)S(1)}) conditional(s32[]{:T(128)} %convert_element_type.477, () %tuple.167, (bf16[4,256,512]{2,1,0:T(8,128)(2,1)}, s32[]{:T(128)}, f32[4,256,1]{1,2,0:T(1,128)}, f32[4,256,2048]{2,1,0:T(8,128)}, f32[4,256,2048]{2,1,0:T(8,128)}, ...), branch_computations={%region_27.27_spmd, %region_28.31_spmd} | conditional | flops 1085013504 | bytes 17583136 | solution.py:150
  430.0 3.4 fusion.62
  435.5 5.5 convolution_bitcast_fusion.1
  441.0 4.6 constant_dynamic-update-slice_fusion.39
  445.7 10.1 %reduce_sum.224 = f32[512,2048]{1,0:T(8,128)} reduce(f32[4,512,2048]{2,1,0:T(8,128)} %get-tuple-element.445, f32[]{:T(128)} %constant.270.clone.1), dimensions={0}, to_apply=%region_33.34 | reduce | flops 3145728 | bytes 20971524 | tf_op jit(solution)/shard_map/reduce_sum | solution.py:199
  455.8 3.8 reduce_sum.225
  462.0 5.8 all-to-all-start.2
  467.8 73.7 %all-reduce = (f32[512]{0:T(512)S(1)}, f32[512]{0:T(512)S(1)}) all-reduce(f32[512]{0:T(512)S(1)} %reduce_sum.226, f32[512]{0:T(512)S(1)} %reduce_sum.227), channel_id=1, replica_groups=mesh['grp'=8,'bal'=16] {'grp','bal'}, use_global_device_ids=true, to_apply=%region_38.39 | all-reduce | flops 1024 | bytes 8192 | tf_op jit(solution)/shard_map/psum | solution.py:272
  544.6 79.3 %all-reduce.4.cloned.1.call-done = (f32[512,2048]{1,0:T(8,128)}, f32[512,512]{1,0:T(8,128)}) async-done(((f32[512,2048]{1,0:T(8,128)}, f32[512,512]{1,0:T(8,128)}), (f32[512,2048]{1,0:T(8,128)}, f32[512,512]{1,0:T(8,128)})) %all-reduce.4.cloned.1.call-update) | async-done | bytes 5242896 | tf_op jit(solution)/shard_map/psum | solution.py:272
  623.9 4.9 broadcast_multiply_fusion.6
  (372 shorter events, 214.9 us)
Async XLA Ops:
  7.2 60.8 %copy-start.36 = (bf16[1,512,512]{2,1,0:T(8,128)(2,1)S(1)}, bf16[1,512,512]{2,1,0:T(8,128)(2,1)}, u32[]{:S(2)}) copy-start(bf16[1,512,512]{2,1,0:T(8,128)(2,1)} %param.22) | copy-start | bytes 1572868
  52.0 16.6 %copy-start.40 = (s32[8]{0:T(128)}, s32[8]{0:T(128)S(1)}, u32[]{:S(2)}) copy-start(s32[8]{0:T(128)S(1)} %fusion.169) | copy-start | bytes 100
  55.1 26.5 %all-to-all-start.1 = ((bf16[16,64,512]{2,1,0:T(8,128)(2,1)}), bf16[16,64,512]{2,1,0:T(8,128)(2,1)S(1)}, u32[]{:S(2)}, u32[]{:S(2)}) async-start(bf16[16,64,512]{2,1,0:T(8,128)(2,1)} %bitcast.70), calls=%async_computation.1 | async-start | bytes 2097152 | tf_op jit(solution)/shard_map/all_to_all | solution.py:248
  67.0 163.3 %copy-start.42 = (s32[16]{0:T(128)}, s32[16]{0:T(128)S(1)}, u32[]{:S(2)}) copy-start(s32[16]{0:T(128)S(1)} %get-tuple-element.578) | copy-start | bytes 196
  81.6 147.0 %all-to-all-start = ((bf16[16,64,512]{2,1,0:T(8,128)(2,1)}), bf16[16,64,512]{2,1,0:T(8,128)(2,1)}, u32[]{:S(2)}, u32[]{:S(2)}) async-start(bf16[16,64,512]{2,1,0:T(8,128)(2,1)} %bitcast.66), calls=%async_computation | async-start | bytes 2097152 | tf_op jit(solution)/shard_map/all_to_all | solution.py:251
  86.6 537.4 %all-reduce.4.cloned.1.call-start = ((), (), s32[]{:S(2)}) async-start(), calls=%async_computation.3 | async-start | bytes 10485760 | tf_op jit(solution)/shard_map/psum | solution.py:272
  87.2 4.8 copy-start
  87.2 4.8 copy-start.30
  186.4 19.1 %copy-start.15 = (f32[1024,1024]{1,0:T(8,128)}, f32[1024,1024]{1,0:T(8,128)S(1)}, u32[]{:S(2)}) copy-start(f32[1024,1024]{1,0:T(8,128)S(1)} %fusion.155) | copy-start | bytes 12582916
  205.5 7.7 %copy-start.8 = (bf16[1024,1024]{1,0:T(8,128)(2,1)}, bf16[1024,1024]{1,0:T(8,128)(2,1)S(1)}, u32[]{:S(2)}) copy-start(bf16[1024,1024]{1,0:T(8,128)(2,1)S(1)} %get-tuple-element.573) | copy-start | bytes 6291460
  205.5 7.7 %copy-start.10 = (bf16[1024,1024]{1,0:T(8,128)(2,1)}, bf16[1024,1024]{1,0:T(8,128)(2,1)S(1)}, u32[]{:S(2)}) copy-start(bf16[1024,1024]{1,0:T(8,128)(2,1)S(1)} %get-tuple-element.574) | copy-start | bytes 6291460
  205.5 7.7 %copy-start.6 = (bf16[1024,1024]{1,0:T(8,128)(2,1)}, bf16[1024,1024]{1,0:T(8,128)(2,1)S(1)}, u32[]{:S(2)}) copy-start(bf16[1024,1024]{1,0:T(8,128)(2,1)S(1)} %get-tuple-element.572) | copy-start | bytes 6291460
  205.5 9.4 %copy-start.12 = (bf16[1024,1024]{1,0:T(8,128)(2,1)}, bf16[1024,1024]{1,0:T(8,128)(2,1)S(1)}, u32[]{:S(2)}) copy-start(bf16[1024,1024]{1,0:T(8,128)(2,1)S(1)} %get-tuple-element.575) | copy-start | bytes 6291460
  205.5 9.4 %copy-start.13 = (bf16[1024,1024]{1,0:T(8,128)(2,1)}, bf16[1024,1024]{1,0:T(8,128)(2,1)S(1)}, u32[]{:S(2)}) copy-start(bf16[1024,1024]{1,0:T(8,128)(2,1)S(1)} %get-tuple-element.569) | copy-start | bytes 6291460
  205.5 20.4 %copy-start.2 = (bf16[1024,1024]{1,0:T(8,128)(2,1)}, bf16[1024,1024]{1,0:T(8,128)(2,1)S(1)}, u32[]{:S(2)}) copy-start(bf16[1024,1024]{1,0:T(8,128)(2,1)S(1)} %get-tuple-element.576) | copy-start | bytes 6291460
  227.7 4.5 copy-start.23
  227.7 4.5 copy-start.24
  230.8 6.4 %copy-start.37 = (f32[512]{0:T(512)S(1)}, f32[512]{0:T(512)}, u32[]{:S(2)}) copy-start(f32[512]{0:T(512)} %param.26) | copy-start | bytes 6148
  272.4 5.3 copy-start.38
  272.4 2.4 copy-start.14
  272.4 4.6 copy-start.11
  274.7 2.9 copy-start.9
  277.0 1.6 copy-start.7
  277.7 1.8 copy-start.5
  278.6 1.7 copy-start.4
  279.4 1.7 copy-start.3
  280.4 2.3 copy-start.22
  282.7 5.2 copy-start.21
  288.0 4.9 copy-start.20
  292.9 4.8 copy-start.19
  297.7 4.9 copy-start.18
  302.6 4.8 copy-start.17
  307.4 4.9 copy-start.16
  312.3 4.8 copy-start.44
  359.1 4.9 copy-start.32
  359.1 5.1 copy-start.33
  359.1 5.2 copy-start.34
  359.1 5.4 copy-start.35
  366.7 2.2 copy-start.26
  366.7 2.4 copy-start.27
  366.8 2.6 copy-start.28
  366.8 2.8 copy-start.29
  372.0 5.8 copy-start.1
  372.0 5.8 copy-start.31
  459.6 0.6 copy-start.43
  459.6 8.2 %copy-start.39 = (f32[4,512]{1,0:T(4,128)S(1)}, f32[4,512]{1,0:T(4,128)}, u32[]{:S(2)}) copy-start(f32[4,512]{1,0:T(4,128)} %copy-done.38) | copy-start | bytes 24580
  460.2 83.1 %copy-start.41 = (s32[8]{0:T(128)S(1)}, s32[8]{0:T(128)}, u32[]{:S(2)}) copy-start(s32[8]{0:T(128)} %copy-done.40) | copy-start | bytes 100
  462.0 80.6 %all-to-all-start.2 = ((bf16[16,64,512]{2,1,0:T(8,128)(2,1)}), bf16[16,64,512]{2,1,0:T(8,128)(2,1)S(1)}, u32[]{:S(2)}, u32[]{:S(2)}) async-start(bf16[16,64,512]{2,1,0:T(8,128)(2,1)} %bitcast.74), calls=%async_computation.2 | async-start | bytes 2097152 | tf_op jit(solution)/shard_map/all_to_all | solution.py:268
  623.9 4.9 copy-start.25
Sparse Core Ops, SparseCore 0:
  459.7 164.1 all-reduce.3
where the time goes:
time: 644 us; the launch traced here: 637 us
  matrix products  205 us (32%)
  local copies, waits for them, and re-layouts  132 us (20%)
  waiting for transfers between devices  90.9 us (14%)
  blocking collectives  73.7 us (11%)
  other arithmetic  70.4 us (11%)
  loops' own time  29.7 us (5%)
  starting transfers between devices  20.1 us (3%)
  between operations  16 us (2%)
    dot_general x24, matrix products, contract_cols(): lax.dot_general(left, right, (((1,), (1,)), ((), ())), preferred_element_...  103 us
    psum x1, waiting for transfers between devices, per_device(): sums = lax.psum((terms[0], terms[1], terms[2], terms[3]), ('grp', 'bal'))  79.3 us
    psum x1, blocking collectives, per_device(): sums = lax.psum((terms[0], terms[1], terms[2], terms[3]), ('grp', 'bal'))  73.7 us
    dynamic_update_slice x48, local copies, waits for them, and re-layouts, held_tiles_map(): return lax.map(each_tile, (jnp.arange(count, dtype=jnp.int32), pieces))  57.7 us
    dot_general x24, matrix products, contract_rows(): lax.dot_general(left, right, (((0,), (0,)), ((), ())), preferred_element_...  51.2 us
    another operation x1, loops' own time, pack_histories(): final_state, ranks = lax.scan(advance, start_state, seq_lengths)  20.9 us
    dynamic_slice x16, local copies, waits for them, and re-layouts, pack_histories(): final_state, ranks = lax.scan(advance, start_state, seq_lengths)  19.9 us
    dot_general x8, matrix products, attend_backward(): jnp.dot(grad_scores, key_head, preferred_element_type=jnp.float32) * scale  19.2 us
  transfers between devices with their start and end apart: 4, of which 2 were waited for; matrix products, arithmetic and copies ran while one was open for 23% of the time, Pallas kernels for 0%

commit v1 on v0

--- a/solution.py
+++ b/solution.py
@@ -269,7 +269,7 @@
         regroup(return_table, d_held), "bal", split_axis=0, concat_axis=0, tiled=True
     )
     d_rows = regroup(home_table, came_back)
-    sums = lax.psum((terms[0], terms[1], terms[2], terms[3]), ("grp", "bal"))
+    sums = lax.psum(lax.psum((terms[0], terms[1], terms[2], terms[3]), "grp"), "bal")
     divisor = float(lax.axis_size("grp") * peers)
     return (
         d_rows[None],

time: 644 us -> 864 us (1.34)
  waiting for transfers between devices: 90.9 us -> 320 us
  blocking collectives: 73.7 us -> 63.3 us
    psum x1 -> x2, waiting for transfers between devices: 79.3 us -> 308 us  [the longest x1 222 us: per_device(): lax.psum((terms[0], terms[1], terms[2], terms[3]), 'grp')]
    psum x1 -> x2, blocking collectives: 73.7 us -> 63.3 us  [the longest x1 35.5 us: per_device(): lax.psum(lax.psum((terms[0], terms[1], terms[2], terms[3]), 'grp'), 'bal')]
  transfers between devices with their start and end apart: 4 -> 5, of which waited for: 2 -> 3; matrix products, arithmetic and copies ran while one was open for 23% -> 17% of each run, Pallas kernels for 0% -> 0%
where the time goes in v1:
time: 864 us; the launch traced here: 857 us
  waiting for transfers between devices  320 us (37%)
  matrix products  205 us (24%)
  local copies, waits for them, and re-layouts  132 us (15%)
  other arithmetic  70.4 us (8%)
  blocking collectives  63.3 us (7%)
  loops' own time  29.7 us (3%)
  starting transfers between devices  21.8 us (3%)
  between operations  16.1 us (2%)
    psum x1, waiting for transfers between devices, per_device(): lax.psum((terms[0], terms[1], terms[2], terms[3]), 'grp')  222 us
    dot_general x24, matrix products, contract_cols(): lax.dot_general(left, right, (((1,), (1,)), ((), ())), preferred_element_...  103 us
    psum x1, waiting for transfers between devices, per_device(): lax.psum(lax.psum((terms[0], terms[1], terms[2], terms[3]), 'grp'), 'bal')  86.2 us
    dynamic_update_slice x48, local copies, waits for them, and re-layouts, held_tiles_map(): return lax.map(each_tile, (jnp.arange(count, dtype=jnp.int32), pieces))  57.7 us
    dot_general x24, matrix products, contract_rows(): lax.dot_general(left, right, (((0,), (0,)), ((), ())), preferred_element_...  51.2 us
    psum x1, blocking collectives, per_device(): lax.psum(lax.psum((terms[0], terms[1], terms[2], terms[3]), 'grp'), 'bal')  35.5 us
    psum x1, blocking collectives, per_device(): lax.psum((terms[0], terms[1], terms[2], terms[3]), 'grp')  27.8 us
    another operation x1, loops' own time, pack_histories(): final_state, ranks = lax.scan(advance, start_state, seq_lengths)  20.9 us
  transfers between devices with their start and end apart: 5, of which 3 were waited for; matrix products, arithmetic and copies ran while one was open for 17% of the time, Pallas kernels for 0%

profile of v1, /device:TPU:1, one launch (start us, length us, event | category | flops | bytes accessed | tf_op | source)
XLA Modules:
  0.0 857.0 jit_solution(7507314394235276217)
XLA Ops:
  7.2 42.6 %while.66 = (s32[]{:T(128)}, s32[]{:T(128)}, s32[]{:T(128)}, s32[16]{0:T(128)S(1)}, s32[16]{0:T(128)}) while((s32[]{:T(128)}, s32[]{:T(128)}, s32[]{:T(128)}, s32[16]{0:T(128)S(1)}, s32[16]{0:T(128)}) %tuple.201), condition=%wide.region_3.4_spmd.clone, body=%wide.region_2.3_spmd.sunk.clone | while | flops 8 | bytes 148 | solution.py:137
  55.1 9.3 %all-to-all-start.1 = ((bf16[16,64,512]{2,1,0:T(8,128)(2,1)}), bf16[16,64,512]{2,1,0:T(8,128)(2,1)S(1)}, u32[]{:S(2)}, u32[]{:S(2)}) async-start(bf16[16,64,512]{2,1,0:T(8,128)(2,1)} %bitcast.70), calls=%async_computation.1 | async-start | bytes 2097152 | tf_op jit(solution)/shard_map/all_to_all | solution.py:248
  70.0 11.6 %all-to-all-done.1 = bf16[16,64,512]{2,1,0:T(8,128)(2,1)S(1)} async-done(((bf16[16,64,512]{2,1,0:T(8,128)(2,1)}), bf16[16,64,512]{2,1,0:T(8,128)(2,1)S(1)}, u32[]{:S(2)}, u32[]{:S(2)}) %all-to-all-start.1) | async-done | bytes 1048608 | tf_op jit(solution)/shard_map/all_to_all | solution.py:248
  81.6 5.0 all-to-all-start
  91.9 70.2 %while.67 = (s32[]{:T(128)}, f32[4,256,512]{2,1,0:T(8,128)}, f32[4,256,1]{1,2,0:T(1,128)}, bf16[4,256,512]{2,1,0:T(8,128)(2,1)}, f32[4,256,2048]{2,1,0:T(8,128)}...) while((s32[]{:T(128)}, f32[4,256,512]{2,1,0:T(8,128)}, ...), condition=%wide.region_16.17_spmd.clone, body=%wide.region_11.16_spmd.sunk.clone | while | flops 541589760 | bytes 17060060 | solution.py:152
  93.2 9.2 %conditional.9 = (f32[1,256,512]{2,1,0:T(8,128)S(1)}, f32[1,256,1]{1,2,0:T(1,128)}, bf16[1,256,512]{2,1,0:T(8,128)(2,1)S(1)}, f32[1,256,2048]{2,1,0:T(8,128)}, bf16[1,256,2048]{2,1,0:T(8,128)(2,1)S(1)}) conditional(s32[]{:T(128)} %convert_element_type.475, () %tuple.157, (bf16[4,256,512]{2,1,0:T(8,128)(2,1)}, s32[]{:T(128)}, f32[512]{0:T(512)S(1)}, ...), branch_computations={%region_12.12_spmd, %region_13.15_spmd} | conditional | flops 541589760 | bytes 9190964 | solution.py:150
  96.0 3.1 fusion.8
  102.4 3.2 constant_dynamic-update-slice_fusion.33
  110.8 9.2 %conditional.9 = (f32[1,256,512]{2,1,0:T(8,128)S(1)}, f32[1,256,1]{1,2,0:T(1,128)}, bf16[1,256,512]{2,1,0:T(8,128)(2,1)S(1)}, f32[1,256,2048]{2,1,0:T(8,128)}, bf16[1,256,2048]{2,1,0:T(8,128)(2,1)S(1)}) conditional(s32[]{:T(128)} %convert_element_type.475, () %tuple.157, (bf16[4,256,512]{2,1,0:T(8,128)(2,1)}, s32[]{:T(128)}, f32[512]{0:T(512)S(1)}, ...), branch_computations={%region_12.12_spmd, %region_13.15_spmd} | conditional | flops 541589760 | bytes 9190964 | solution.py:150
  113.6 3.1 fusion.8
  120.0 3.1 constant_dynamic-update-slice_fusion.33
  128.4 9.2 %conditional.9 = (f32[1,256,512]{2,1,0:T(8,128)S(1)}, f32[1,256,1]{1,2,0:T(1,128)}, bf16[1,256,512]{2,1,0:T(8,128)(2,1)S(1)}, f32[1,256,2048]{2,1,0:T(8,128)}, bf16[1,256,2048]{2,1,0:T(8,128)(2,1)S(1)}) conditional(s32[]{:T(128)} %convert_element_type.475, () %tuple.157, (bf16[4,256,512]{2,1,0:T(8,128)(2,1)}, s32[]{:T(128)}, f32[512]{0:T(512)S(1)}, ...), branch_computations={%region_12.12_spmd, %region_13.15_spmd} | conditional | flops 541589760 | bytes 9190964 | solution.py:150
  131.2 3.1 fusion.8
  137.6 3.2 constant_dynamic-update-slice_fusion.33
  145.9 9.2 %conditional.9 = (f32[1,256,512]{2,1,0:T(8,128)S(1)}, f32[1,256,1]{1,2,0:T(1,128)}, bf16[1,256,512]{2,1,0:T(8,128)(2,1)S(1)}, f32[1,256,2048]{2,1,0:T(8,128)}, bf16[1,256,2048]{2,1,0:T(8,128)(2,1)S(1)}) conditional(s32[]{:T(128)} %convert_element_type.475, () %tuple.157, (bf16[4,256,512]{2,1,0:T(8,128)(2,1)}, s32[]{:T(128)}, f32[512]{0:T(512)S(1)}, ...), branch_computations={%region_12.12_spmd, %region_13.15_spmd} | conditional | flops 541589760 | bytes 9190964 | solution.py:150
  148.8 3.1 fusion.8
  155.2 3.1 constant_dynamic-update-slice_fusion.33
  162.2 3.7 fusion.113
  165.9 3.7 fusion.120
  169.6 3.7 fusion.127
  173.3 3.9 fusion.134
  177.2 3.7 fusion.141
  180.9 3.8 fusion.148
  186.4 19.1 %select_convert_fusion.8 = (bf16[1024,1024]{1,0:T(8,128)(2,1)S(1)}, bf16[1024,1024]{1,0:T(8,128)(2,1)}, bf16[1024,1024]{1,0:T(8,128)(2,1)}, bf16[1024,1024]{1,0:...) fusion(pred[1024]{0:T(1024)(128)(4,1)S(1)} %broadcast_compare_f, ...), kind=kOutput, calls=%fused_computation.122 | convolution fusion | flops 197132288 | bytes 50865152 | tf_op jit(solution)/shard_map/dot_general | solution.py:40
  237.3 35.1 %while.68 = (s32[]{:T(128)}, f32[4,256,512]{2,1,0:T(8,128)}, bf16[4,256,512]{2,1,0:T(8,128)(2,1)}, f32[4,512,512]{2,1,0:T(8,128)}, f32[4,512]{1,0:T(4,128)S(1)},...) while((s32[]{:T(128)}, f32[4,256,512]{2,1,0:T(8,128)}, ...), condition=%wide.region_25.26_spmd.clone, body=%wide.region_17.25_spmd.sunk.clone | while | flops 273415936 | bytes 9736943 | solution.py:152
  238.5 4.9 conditional.10
  247.3 4.9 conditional.10
  256.1 4.9 conditional.10
  264.8 4.9 conditional.10
  282.7 5.2 select_convert_fusion.1
  288.0 4.9 select_convert_fusion.2
  292.9 4.8 select_convert_fusion.3
  297.7 4.9 select_convert_fusion.4
  302.6 4.8 select_convert_fusion.5
  307.4 4.9 select_convert_fusion.6
  312.3 4.8 select_convert_fusion.7
  317.2 4.9 select_convert_fusion
  347.5 2.5 fusion.72
  372.0 5.6 pad_maximum_fusion
  377.8 67.9 %while.69 = (s32[]{:T(128)}, bf16[4,256,512]{2,1,0:T(8,128)(2,1)S(1)}, f32[4,512,2048]{2,1,0:T(8,128)}, f32[4,512]{1,0:T(4,128)S(1)}, s32[4]{0:T(128)S(1)}, /*in...) while((s32[]{:T(128)}, ...), condition=%wide.region_32.33_spmd.clone, body=%wide.region_26.32_spmd.sunk.clone | while | flops 1085013504 | bytes 26500880 | solution.py:152
  379.3 10.9 %conditional.11 = (bf16[1,256,512]{2,1,0:T(8,128)(2,1)S(1)}, f32[1,512,2048]{2,1,0:T(8,128)}, f32[1,512]{1,0:T(1,128)S(1)}) conditional(s32[]{:T(128)} %convert_element_type.477, () %tuple.167, (bf16[4,256,512]{2,1,0:T(8,128)(2,1)}, s32[]{:T(128)}, f32[4,256,1]{1,2,0:T(1,128)}, f32[4,256,2048]{2,1,0:T(8,128)}, f32[4,256,2048]{2,1,0:T(8,128)}, ...), branch_computations={%region_27.27_spmd, %region_28.31_spmd} | conditional | flops 1085013504 | bytes 17583136 | solution.py:150
  379.3 3.4 fusion.62
  384.7 5.5 convolution_bitcast_fusion.1
  390.2 4.6 constant_dynamic-update-slice_fusion.39
  396.1 10.9 %conditional.11 = (bf16[1,256,512]{2,1,0:T(8,128)(2,1)S(1)}, f32[1,512,2048]{2,1,0:T(8,128)}, f32[1,512]{1,0:T(1,128)S(1)}) conditional(s32[]{:T(128)} %convert_element_type.477, () %tuple.167, (bf16[4,256,512]{2,1,0:T(8,128)(2,1)}, s32[]{:T(128)}, f32[4,256,1]{1,2,0:T(1,128)}, f32[4,256,2048]{2,1,0:T(8,128)}, f32[4,256,2048]{2,1,0:T(8,128)}, ...), branch_computations={%region_27.27_spmd, %region_28.31_spmd} | conditional | flops 1085013504 | bytes 17583136 | solution.py:150
  396.2 3.4 fusion.62
  401.6 5.5 convolution_bitcast_fusion.1
  407.1 4.7 constant_dynamic-update-slice_fusion.39
  413.1 11.0 %conditional.11 = (bf16[1,256,512]{2,1,0:T(8,128)(2,1)S(1)}, f32[1,512,2048]{2,1,0:T(8,128)}, f32[1,512]{1,0:T(1,128)S(1)}) conditional(s32[]{:T(128)} %convert_element_type.477, () %tuple.167, (bf16[4,256,512]{2,1,0:T(8,128)(2,1)}, s32[]{:T(128)}, f32[4,256,1]{1,2,0:T(1,128)}, f32[4,256,2048]{2,1,0:T(8,128)}, f32[4,256,2048]{2,1,0:T(8,128)}, ...), branch_computations={%region_27.27_spmd, %region_28.31_spmd} | conditional | flops 1085013504 | bytes 17583136 | solution.py:150
  413.1 3.4 fusion.62
  418.5 5.5 convolution_bitcast_fusion.1
  424.0 4.7 constant_dynamic-update-slice_fusion.39
  430.0 11.0 %conditional.11 = (bf16[1,256,512]{2,1,0:T(8,128)(2,1)S(1)}, f32[1,512,2048]{2,1,0:T(8,128)}, f32[1,512]{1,0:T(1,128)S(1)}) conditional(s32[]{:T(128)} %convert_element_type.477, () %tuple.167, (bf16[4,256,512]{2,1,0:T(8,128)(2,1)}, s32[]{:T(128)}, f32[4,256,1]{1,2,0:T(1,128)}, f32[4,256,2048]{2,1,0:T(8,128)}, f32[4,256,2048]{2,1,0:T(8,128)}, ...), branch_computations={%region_27.27_spmd, %region_28.31_spmd} | conditional | flops 1085013504 | bytes 17583136 | solution.py:150
  430.0 3.4 fusion.62
  435.5 5.5 convolution_bitcast_fusion.1
  441.0 4.6 constant_dynamic-update-slice_fusion.39
  445.7 10.1 %reduce_sum.224 = f32[512,2048]{1,0:T(8,128)} reduce(f32[4,512,2048]{2,1,0:T(8,128)} %get-tuple-element.445, f32[]{:T(128)} %constant.270.clone.1), dimensions={0}, to_apply=%region_33.34 | reduce | flops 3145728 | bytes 20971524 | tf_op jit(solution)/shard_map/reduce_sum | solution.py:199
  455.8 3.7 reduce_sum.225
  459.6 221.8 %all-reduce.9.cloned.1.call-done = (f32[512,2048]{1,0:T(8,128)}, f32[512,512]{1,0:T(8,128)}) async-done(((f32[512,2048]{1,0:T(8,128)}, f32[512,512]{1,0:T(8,128)}), (f32[512,2048]{1,0:T(8,128)}, f32[512,512]{1,0:T(8,128)})) %all-reduce.9.cloned.1.call-update) | async-done | bytes 5242896 | tf_op jit(solution)/shard_map/psum | solution.py:272
  683.9 7.4 all-to-all-start.2
  691.4 27.8 %all-reduce.2 = (f32[512]{0:T(512)S(1)}, f32[512]{0:T(512)S(1)}) all-reduce(f32[512]{0:T(512)S(1)} %reduce_sum.226, f32[512]{0:T(512)S(1)} %reduce_sum.227), channel_id=1, replica_groups=mesh['grp'=8,'bal'=16] {'grp'}, use_global_device_ids=true, to_apply=%region_40.41 | all-reduce | flops 1024 | bytes 8192 | tf_op jit(solution)/shard_map/psum | solution.py:272
  719.2 35.5 %all-reduce = (f32[512]{0:T(512)S(1)}, f32[512]{0:T(512)S(1)}) all-reduce(f32[512]{0:T(512)S(1)} %get-tuple-element.559, f32[512]{0:T(512)S(1)} %get-tuple-element.560), channel_id=1, replica_groups=mesh['grp'=8,'bal'=16] {'bal'}, use_global_device_ids=true, to_apply=%region_41.42 | all-reduce | flops 1024 | bytes 8192 | tf_op jit(solution)/shard_map/psum | solution.py:272
  757.9 86.2 %all-reduce.7.cloned.1.call-done = (f32[512,2048]{1,0:T(8,128)}, f32[512,512]{1,0:T(8,128)}) async-done(((f32[512,2048]{1,0:T(8,128)}, f32[512,512]{1,0:T(8,128)}), (f32[512,2048]{1,0:T(8,128)}, f32[512,512]{1,0:T(8,128)})) %all-reduce.7.cloned.1.call-update) | async-done | bytes 5242896 | tf_op jit(solution)/shard_map/psum | solution.py:272
  844.0 4.9 broadcast_multiply_fusion.6
  (376 shorter events, 219.9 us)
Async XLA Ops:
  7.2 60.8 %copy-start.36 = (bf16[1,512,512]{2,1,0:T(8,128)(2,1)S(1)}, bf16[1,512,512]{2,1,0:T(8,128)(2,1)}, u32[]{:S(2)}) copy-start(bf16[1,512,512]{2,1,0:T(8,128)(2,1)} %param.22) | copy-start | bytes 1572868
  52.0 16.6 %copy-start.40 = (s32[8]{0:T(128)}, s32[8]{0:T(128)S(1)}, u32[]{:S(2)}) copy-start(s32[8]{0:T(128)S(1)} %fusion.169) | copy-start | bytes 100
  55.1 26.5 %all-to-all-start.1 = ((bf16[16,64,512]{2,1,0:T(8,128)(2,1)}), bf16[16,64,512]{2,1,0:T(8,128)(2,1)S(1)}, u32[]{:S(2)}, u32[]{:S(2)}) async-start(bf16[16,64,512]{2,1,0:T(8,128)(2,1)} %bitcast.70), calls=%async_computation.1 | async-start | bytes 2097152 | tf_op jit(solution)/shard_map/all_to_all | solution.py:248
  67.0 163.3 %copy-start.42 = (s32[16]{0:T(128)}, s32[16]{0:T(128)S(1)}, u32[]{:S(2)}) copy-start(s32[16]{0:T(128)S(1)} %get-tuple-element.582) | copy-start | bytes 196
  81.6 147.0 %all-to-all-start = ((bf16[16,64,512]{2,1,0:T(8,128)(2,1)}), bf16[16,64,512]{2,1,0:T(8,128)(2,1)}, u32[]{:S(2)}, u32[]{:S(2)}) async-start(bf16[16,64,512]{2,1,0:T(8,128)(2,1)} %bitcast.66), calls=%async_computation | async-start | bytes 2097152 | tf_op jit(solution)/shard_map/all_to_all | solution.py:251
  86.6 594.9 %all-reduce.9.cloned.1.call-start = ((), (), s32[]{:S(2)}) async-start(), calls=%async_computation.4 | async-start | bytes 10485760 | tf_op jit(solution)/shard_map/psum | solution.py:272
  87.2 4.8 copy-start
  87.2 4.8 copy-start.30
  186.4 19.1 %copy-start.15 = (f32[1024,1024]{1,0:T(8,128)}, f32[1024,1024]{1,0:T(8,128)S(1)}, u32[]{:S(2)}) copy-start(f32[1024,1024]{1,0:T(8,128)S(1)} %fusion.155) | copy-start | bytes 12582916
  205.5 7.7 copy-start.8
  205.5 7.7 copy-start.10
  205.5 7.7 copy-start.6
  205.5 9.4 %copy-start.12 = (bf16[1024,1024]{1,0:T(8,128)(2,1)}, bf16[1024,1024]{1,0:T(8,128)(2,1)S(1)}, u32[]{:S(2)}) copy-start(bf16[1024,1024]{1,0:T(8,128)(2,1)S(1)} %get-tuple-element.579) | copy-start | bytes 6291460
  205.5 9.4 %copy-start.13 = (bf16[1024,1024]{1,0:T(8,128)(2,1)}, bf16[1024,1024]{1,0:T(8,128)(2,1)S(1)}, u32[]{:S(2)}) copy-start(bf16[1024,1024]{1,0:T(8,128)(2,1)S(1)} %get-tuple-element.573) | copy-start | bytes 6291460
  205.5 20.4 %copy-start.2 = (bf16[1024,1024]{1,0:T(8,128)(2,1)}, bf16[1024,1024]{1,0:T(8,128)(2,1)S(1)}, u32[]{:S(2)}) copy-start(bf16[1024,1024]{1,0:T(8,128)(2,1)S(1)} %get-tuple-element.580) | copy-start | bytes 6291460
  227.7 4.5 copy-start.23
  227.7 4.5 copy-start.24
  230.8 6.4 copy-start.37
  272.4 5.3 copy-start.38
  272.4 2.4 copy-start.14
  272.4 4.6 copy-start.11
  274.7 2.9 copy-start.9
  277.0 1.6 copy-start.7
  277.7 1.8 copy-start.5
  278.6 1.7 copy-start.4
  279.4 1.7 copy-start.3
  280.4 2.3 copy-start.22
  282.7 5.2 copy-start.21
  288.0 4.9 copy-start.20
  292.9 4.8 copy-start.19
  297.7 4.9 copy-start.18
  302.6 4.8 copy-start.17
  307.4 4.9 copy-start.16
  312.3 4.8 copy-start.44
  359.1 4.9 copy-start.32
  359.1 5.1 copy-start.33
  359.1 5.2 copy-start.34
  359.1 5.4 copy-start.35
  366.7 2.2 copy-start.26
  366.7 2.4 copy-start.27
  366.8 2.6 copy-start.28
  366.8 2.8 copy-start.29
  372.0 5.8 copy-start.1
  372.0 5.8 copy-start.31
  459.6 222.5 %copy-start.43 = (s32[16]{0:T(128)S(1)}, s32[16]{0:T(128)}, u32[]{:S(2)}) copy-start(s32[16]{0:T(128)} %copy-done.42) | copy-start | bytes 196
  459.6 384.4 %all-reduce.7.cloned.1.call-start = ((), (), s32[]{:S(2)}) async-start(), calls=%async_computation.3 | async-start | bytes 10485760 | tf_op jit(solution)/shard_map/psum | solution.py:272
  681.5 9.9 %copy-start.39 = (f32[4,512]{1,0:T(4,128)S(1)}, f32[4,512]{1,0:T(4,128)}, u32[]{:S(2)}) copy-start(f32[4,512]{1,0:T(4,128)} %copy-done.38) | copy-start | bytes 24580
  682.0 74.4 %copy-start.41 = (s32[8]{0:T(128)S(1)}, s32[8]{0:T(128)}, u32[]{:S(2)}) copy-start(s32[8]{0:T(128)} %copy-done.40) | copy-start | bytes 100
  683.9 72.0 %all-to-all-start.2 = ((bf16[16,64,512]{2,1,0:T(8,128)(2,1)}), bf16[16,64,512]{2,1,0:T(8,128)(2,1)S(1)}, u32[]{:S(2)}, u32[]{:S(2)}) async-start(bf16[16,64,512]{2,1,0:T(8,128)(2,1)} %bitcast.74), calls=%async_computation.2 | async-start | bytes 2097152 | tf_op jit(solution)/shard_map/all_to_all | solution.py:268
  844.0 4.9 copy-start.25
Sparse Core Ops, SparseCore 0:
  459.7 221.7 all-reduce.8
  684.0 159.9 all-reduce.6
